TPU v7x, 32 devices: a whole 2x2x4 slice. The times are simulated.
32 devices in a mesh: wide: 16 (over z, x, core), narrow: 2 (over y).
Axes of the slice: x: 2, y: 2, z: 4, core: 2. Of those that a mesh axis runs over, the one named last changes fastest.
Arguments:
- query_rows: bfloat16 [640, 6144], P('wide', 'narrow'), may hold values from -30 to 30
- key_rows: bfloat16 [640, 6144], P('wide', 'narrow'), may hold values from -10 to 10
- value_rows: bfloat16 [640, 6144], P('wide', 'narrow'), may hold values from -6 to 6
- mid_grad: bfloat16 [5120, 2048], P(('wide', 'narrow')), may hold values from -6 to 6
- link_weight: bfloat16 [768, 2048], replicated, may hold values from -0.21875 to 0.21875
Outputs:
- query_grad: bfloat16 [640, 6144], P('wide', 'narrow')
- key_grad: bfloat16 [640, 6144], P('wide', 'narrow')
- value_grad: bfloat16 [640, 6144], P('wide', 'narrow')
All inputs are finite; a program needn't handle non-finite values.
Results may differ from a plain program's by a relative error of at most 0.0066.
Values may be sent and summed in bfloat16 or wider, within the bound.
No kernel may reach another device: no remote copies, remote signals or barrier semaphores. Data moves between devices by JAX's collectives and lax.ppermute only.
A program may use at most 64 MiB of HBM per device.

v0:
```python
import math
import jax
import jax.numpy as jnp
from jax import lax
from jax.sharding import PartitionSpec as P

HD = 128
PATCH = 8
lowest = -1e30


def on_device(query_rows, key_rows, value_rows, mid_grad, link_weight):
    groups = lax.axis_size("narrow")
    patches = query_rows.shape[0]
    columns = query_rows.shape[1]
    heads_here = columns // HD
    scaling = 1.0 / math.sqrt(HD)
    local_patches = mid_grad.shape[0] // PATCH
    grouped = mid_grad.reshape(local_patches, groups, PATCH // groups, mid_grad.shape[1])
    moved = jnp.einsum(
        "abcm,pm->abcp",
        lax.all_to_all(grouped, "narrow", split_axis=1, concat_axis=0, tiled=True),
        link_weight,
        preferred_element_type=jnp.float32,
    ).astype(jnp.bfloat16)
    incoming = moved.reshape(patches, columns)
    incoming_heads = incoming.reshape(patches, heads_here, HD)
    query_heads = query_rows.reshape(patches, heads_here, HD)
    key_heads = key_rows.reshape(patches, heads_here, HD)
    value_heads = value_rows.reshape(patches, heads_here, HD)
    own_pos = lax.axis_index("wide") * patches + jnp.arange(patches, dtype=jnp.int32)
    total_rows = patches * lax.axis_size("wide")
    empty_store = jnp.zeros((total_rows, columns), jnp.bfloat16)
    fold_start = (
        jnp.full((heads_here, patches), lowest, jnp.float32),
        jnp.zeros((heads_here, patches), jnp.float32),
        jnp.zeros((heads_here, patches), jnp.float32),
        empty_store,
        empty_store,
    )
    pieces = (
        lax.all_gather(key_rows, "wide", axis=0, tiled=True),
        lax.all_gather(value_rows, "wide", axis=0, tiled=True),
    )
    key_piece, value_piece = pieces
    piece_rows = key_piece.shape[0]
    key_split = key_piece.reshape(piece_rows, heads_here, HD)
    value_split = value_piece.reshape(piece_rows, heads_here, HD)
    piece_pos = jnp.arange(piece_rows, dtype=jnp.int32)
    allowed = piece_pos[None, None, :] <= own_pos[None, :, None]
    scores = (
        jnp.einsum("qhd,khd->hqk", query_heads, key_split, preferred_element_type=jnp.float32)
        * scaling
    )
    scores = jnp.where(allowed, scores, lowest)
    products = jnp.einsum(
        "qhd,khd->hqk", incoming_heads, value_split, preferred_element_type=jnp.float32
    )
    old_max, old_total, old_tilt = fold_start[:3]
    new_max = jnp.maximum(old_max, jnp.max(scores, axis=2))
    expo = jnp.where(allowed, jnp.exp(scores - new_max[:, :, None]), 0.0)
    stats = (new_max, jnp.sum(expo, axis=2), jnp.sum(expo * products, axis=2))
    key_store = pieces[0]
    value_store = pieces[1]
    folded = stats + (key_store, value_store)
    run_max, run_total, run_tilt = (folded[0], folded[1], folded[2])
    log_total = run_max + jnp.log(run_total)
    row_delta = run_tilt / run_total
    key_all = folded[3].reshape(total_rows, heads_here, HD)
    value_all = folded[4].reshape(total_rows, heads_here, HD)
    every_pos = jnp.arange(total_rows, dtype=jnp.int32)
    allowed_q = every_pos[None, None, :] <= own_pos[None, :, None]
    scores_q = (
        jnp.einsum("qhd,khd->hqk", query_heads, key_all, preferred_element_type=jnp.float32)
        * scaling
    )
    products_q = jnp.einsum(
        "qhd,khd->hqk", incoming_heads, value_all, preferred_element_type=jnp.float32
    )
    weights_q = jnp.where(
        allowed_q, jnp.exp(jnp.where(allowed_q, scores_q, lowest) - log_total[:, :, None]), 0.0
    )
    score_grad_q = (weights_q * (products_q - row_delta[:, :, None])).astype(jnp.bfloat16)
    query_accum = jnp.einsum(
        "hqk,khd->qhd", score_grad_q, key_all, preferred_element_type=jnp.float32
    )
    query_grad = (query_accum * scaling).astype(jnp.bfloat16).reshape(patches, columns)
    total_all, delta_all = (
        lax.all_gather(log_total, "wide", axis=1, tiled=True),
        lax.all_gather(row_delta, "wide", axis=1, tiled=True),
    )
    query_piece = lax.all_gather(query_rows, "wide", axis=0, tiled=True)
    grad_piece = lax.all_gather(incoming, "wide", axis=0, tiled=True)
    piece_rows = query_piece.shape[0]
    query_split = query_piece.reshape(piece_rows, heads_here, HD)
    grad_split = grad_piece.reshape(piece_rows, heads_here, HD)
    piece_pos = jnp.arange(piece_rows, dtype=jnp.int32)
    allowed = own_pos[None, None, :] <= piece_pos[None, :, None]
    scores = (
        jnp.einsum("qhd,khd->hqk", query_split, key_heads, preferred_element_type=jnp.float32)
        * scaling
    )
    scores = jnp.where(allowed, scores, lowest)
    products = jnp.einsum(
        "qhd,khd->hqk", grad_split, value_heads, preferred_element_type=jnp.float32
    )
    weights = jnp.where(allowed, jnp.exp(scores - total_all[:, :, None]), 0.0)
    score_grad = (weights * (products - delta_all[:, :, None])).astype(jnp.bfloat16)
    key_accum = jnp.einsum(
        "hqk,qhd->khd", score_grad, query_split, preferred_element_type=jnp.float32
    )
    value_accum = jnp.einsum(
        "hqk,qhd->khd", weights.astype(jnp.bfloat16), grad_split, preferred_element_type=jnp.float32
    )
    key_accum, value_accum = (key_accum, value_accum)
    key_grad = (key_accum * scaling).astype(jnp.bfloat16).reshape(patches, columns)
    value_grad = value_accum.astype(jnp.bfloat16).reshape(patches, columns)
    return (query_grad, key_grad, value_grad)


def solution(mesh):
    in_specs = (
        P("wide", "narrow"),
        P("wide", "narrow"),
        P("wide", "narrow"),
        P(("wide", "narrow"), None),
        P(),
    )
    out_specs = (P("wide", "narrow"), P("wide", "narrow"), P("wide", "narrow"))
    return jax.shard_map(
        on_device, mesh=mesh, in_specs=in_specs, out_specs=out_specs, check_vma=False
    )
```

profile of v0, /device:TPU:0, one launch (start us, length us, event | category | flops | bytes accessed | tf_op | source)
XLA Modules:
  0.0 240.6 jit_solution(15646590345335519802)
XLA Ops:
  7.2 0.7 all-gather.7.cloned.1.call-update
  8.0 0.7 all-gather.9.cloned.1.call-update
  8.7 0.7 all-gather.11.cloned.1.call-update
  9.4 2.3 reshape.125
  11.7 1.4 copy.35
  13.1 13.4 %all_to_all.15 = bf16[20,2,4,2048]{3,2,0,1:T(4,128)(2,1)S(1)} all-to-all(bf16[20,2,4,2048]{3,2,0,1:T(4,128)(2,1)S(1)} %copy.35), channel_id=1, replica_groups=mesh['wide'=16,'narrow'=2] {'narrow'}, dimensions={1} | all-to-all | bytes 1310720 | tf_op jit(solution)/shard_map/all_to_all | solution.py:22
  26.6 1.5 fusion.25
  28.0 0.7 copy.67
  28.8 0.1 iota_compare_fusion.1
  29.0 0.8 copy.37
  29.8 1.7 reshape_reshape.3
  31.5 30.6 %all-gather.7.cloned.1.call-done = bf16[640,3072]{1,0:T(8,128)(2,1)} async-done(((bf16[40,3072]{1,0:T(8,128)(2,1)}), bf16[640,3072]{1,0:T(8,128)(2,1)}) %all-gather.7.cloned.1.call-update) | async-done | bytes 3932176 | tf_op jit(solution)/shard_map/all_gather | solution.py:42
  62.1 6.3 %copy.32 = bf16[640,3072]{0,1:T(8,128)(2,1)} copy(bf16[640,3072]{1,0:T(8,128)(2,1)} %all-gather.7.cloned.1.call-done) | data formatting | bytes 7864320 | tf_op jit(solution)/shard_map/all_gather | solution.py:42
  68.4 43.6 %all-gather.9.cloned.1.call-done = bf16[640,3072]{1,0:T(8,128)(2,1)} async-done(((bf16[40,3072]{1,0:T(8,128)(2,1)}), bf16[640,3072]{1,0:T(8,128)(2,1)}) %all-gather.9.cloned.1.call-update) | async-done | bytes 3932176 | tf_op jit(solution)/shard_map/all_gather | solution.py:43
  112.0 6.2 %copy.38 = bf16[640,3072]{0,1:T(8,128)(2,1)} copy(bf16[640,3072]{1,0:T(8,128)(2,1)} %all-gather.9.cloned.1.call-done) | data formatting | bytes 7864320 | tf_op jit(solution)/shard_map/all_gather | solution.py:43
  118.3 3.3 %fusion.57 = (f32[24,40]{1,0:T(8,128)S(1)}, f32[24,40,640]{2,1,0:T(8,128)S(1)}) fusion(bf16[640,24,128]{0,2,1:T(8,128)(2,1)} %bitcast.76, pred[40,640]{1,0:T(8,128)(4,1)S(1)} %iota_compare_fusion.1, bf16[40,3072]{1,0:T(8,128)(2,1)S(1)} %copy-done.3), kind=kOutput, calls=%fused_computation.62 | convolution fusion | flops 159128640 | bytes 6664960 | tf_op jit(solution)/shard_map/qhd,khd->hqk/dot_general | solution.py:74
  121.6 0.2 copy-done.2
  121.8 1.4 fusion.2
  123.2 0.7 copy-done.1
  123.9 1.8 fusion.33
  125.7 0.7 copy.94
  126.4 19.6 %all-gather = f32[16,40,24]{1,2,0:T(8,128)S(1)} all-gather(f32[1,40,24]{1,2,0:T(8,128)S(1)} %bitcast.88), channel_id=1, replica_groups=mesh['wide'=16,'narrow'=2] {'wide'}, dimensions={0}, use_global_device_ids=true | all-gather | bytes 65280 | tf_op jit(solution)/shard_map/all_gather | solution.py:89
  146.1 0.1 reshape.137
  146.2 18.5 %all-gather.1 = f32[16,40,24]{1,2,0:T(8,128)S(1)} all-gather(f32[1,40,24]{1,2,0:T(8,128)S(1)} %bitcast.87), channel_id=1, replica_groups=mesh['wide'=16,'narrow'=2] {'wide'}, dimensions={0}, use_global_device_ids=true | all-gather | bytes 65280 | tf_op jit(solution)/shard_map/all_gather | solution.py:90
  164.7 0.1 reshape.139
  164.9 6.4 %copy.43 = bf16[640,3072]{0,1:T(8,128)(2,1)} copy(bf16[640,3072]{1,0:T(8,128)(2,1)} %all-gather.11.cloned.1.call-done) | data formatting | bytes 7864320 | tf_op jit(solution)/shard_map/all_gather | solution.py:92
  171.4 4.5 %fusion.43 = f32[24,640,40]{1,2,0:T(8,128)} fusion(bf16[640,24,128]{0,2,1:T(8,128)(2,1)} %bitcast.78, bf16[40,3072]{1,0:T(8,128)(2,1)S(1)} %copy-done.4), kind=kOutput, calls=%fused_computation.43 | convolution fusion | flops 157286400 | bytes 6635520 | tf_op jit(solution)/shard_map/qhd,khd->hqk/dot_general | solution.py:100
  175.9 37.4 %all-gather.13.cloned.1.call-done = bf16[640,3072]{1,0:T(8,128)(2,1)} async-done(((bf16[40,3072]{1,0:T(8,128)(2,1)}), bf16[640,3072]{1,0:T(8,128)(2,1)}) %all-gather.13.cloned.1.call-update) | async-done | bytes 3932176 | tf_op jit(solution)/shard_map/all_gather | solution.py:93
  213.3 6.3 %copy.48 = bf16[640,3072]{0,1:T(8,128)(2,1)} copy(bf16[640,3072]{1,0:T(8,128)(2,1)} %all-gather.13.cloned.1.call-done) | data formatting | bytes 7864320 | tf_op jit(solution)/shard_map/all_gather | solution.py:93
  219.6 5.3 %fusion.35 = bf16[24,5,8,128]{3,2,1,0:T(8,128)(2,1)} fusion(bf16[640,24,128]{0,2,1:T(8,128)(2,1)} %bitcast.81, f32[24,640,40]{1,2,0:T(8,128)} %fusion.43, f32[24,640]{1,0:T(8,128)S(1)} %bitcast.89, pred[640,40]{0,1:T(8,128)(4,1)S(1)} %iota_compare_fusion), kind=kOutput, calls=%fused_computation.36 | convolution fusion | flops 160481280 | bytes 6722560 | tf_op jit(solution)/shard_map/hqk,qhd->khd/dot_general | solution.py:112
  224.9 7.3 %fusion.34 = bf16[24,5,8,128]{3,2,1,0:T(8,128)(2,1)} fusion(bf16[640,24,128]{0,2,1:T(8,128)(2,1)} %bitcast.79, f32[24,640,40]{1,2,0:T(8,128)} %fusion.43, bf16[640,24,128]{0,2,1:T(8,128)(2,1)} %bitcast.82, f32[24,640]{1,0:T(8,128)S(1)} %bitcast.91, f32[24,640]{1,0:T(8,128)S(1)} %bitcast.90, pred[640,40]{0,1:T(8,128)(4,1)S(1)} %iota_compare_fusion, ...), kind=kOutput, calls=%fused_computation.35 | convolution fusion | flops 319119360 | bytes 10961920 | tf_op jit(solution)/shard_map/hqk,qhd->khd/dot_general | solution.py:109
  232.1 1.9 copy_bitcast_fusion
  (24 shorter events, 0.4 us)
Async XLA Ops:
  7.2 19.4 %copy-start = (bf16[768,2048]{1,0:T(8,128)(2,1)S(1)}, bf16[768,2048]{1,0:T(8,128)(2,1)}, u32[]{:S(2)}) copy-start(bf16[768,2048]{1,0:T(8,128)(2,1)} %param.9) | copy-start | bytes 9437188
  7.2 54.9 %all-gather.7.cloned.1.call-start = ((), (), s32[]{:S(2)}) async-start(), calls=%async_computation.1 | async-start | bytes 4177920 | tf_op jit(solution)/shard_map/all_gather | solution.py:42
  7.9 104.1 %all-gather.9.cloned.1.call-start = ((), (), s32[]{:S(2)}) async-start(), calls=%async_computation.2 | async-start | bytes 4177920 | tf_op jit(solution)/shard_map/all_gather | solution.py:43
  8.7 156.2 %all-gather.11.cloned.1.call-start = ((), (), s32[]{:S(2)}) async-start(), calls=%async_computation.3 | async-start | bytes 4177920 | tf_op jit(solution)/shard_map/all_gather | solution.py:92
  9.4 203.9 %all-gather.13.cloned.1.call-start = ((), (), s32[]{:S(2)}) async-start(), calls=%async_computation.4 | async-start | bytes 4177920 | tf_op jit(solution)/shard_map/all_gather | solution.py:93
  68.4 49.9 %copy-start.3 = (bf16[40,3072]{1,0:T(8,128)(2,1)S(1)}, bf16[40,3072]{1,0:T(8,128)(2,1)}, u32[]{:S(2)}) copy-start(bf16[40,3072]{1,0:T(8,128)(2,1)} %param.5) | copy-start | bytes 737284
  118.3 3.5 %copy-start.2 = (bf16[640,3072]{0,1:T(8,128)(2,1)S(1)}, bf16[640,3072]{0,1:T(8,128)(2,1)}, u32[]{:S(2)}) copy-start(bf16[640,3072]{0,1:T(8,128)(2,1)} %copy.38) | copy-start | bytes 11796484
  118.3 3.5 %copy-start.5 = (bf16[40,24,128]{2,1,0:T(8,128)(2,1)S(1)}, bf16[40,24,128]{2,1,0:T(8,128)(2,1)}, u32[]{:S(2)}) copy-start(bf16[40,24,128]{2,1,0:T(8,128)(2,1)} %reshape_reshape.3) | copy-start | bytes 737284
  121.8 2.1 copy-start.1
  164.9 6.5 %copy-start.4 = (bf16[40,3072]{1,0:T(8,128)(2,1)S(1)}, bf16[40,3072]{1,0:T(8,128)(2,1)}, u32[]{:S(2)}) copy-start(bf16[40,3072]{1,0:T(8,128)(2,1)} %param.6) | copy-start | bytes 737284
  219.6 5.3 %copy-start.6 = (bf16[40,3072]{1,0:T(8,128)(2,1)S(1)}, bf16[40,3072]{1,0:T(8,128)(2,1)}, u32[]{:S(2)}) copy-start(bf16[40,3072]{1,0:T(8,128)(2,1)} %param.7) | copy-start | bytes 737284
Sparse Core Ops, SparseCore 0:
  10.3 51.7 all-gather.6
  64.3 47.6 all-gather.8
  114.3 48.4 all-gather.10
  164.9 48.3 all-gather.12
where the time goes:
time: 241 us
  waiting for transfers between devices  114 us (47%)
  blocking collectives  51.5 us (21%)
  local copies, waits for them, and re-layouts  36.1 us (15%)
  matrix products  25 us (10%)
  between operations  13.9 us (6%)
    all_gather x1, waiting for transfers between devices, on_device(): lax.all_gather(value_rows, 'wide', axis=0, tiled=True)  43.6 us
    all_gather x1, waiting for transfers between devices, on_device(): grad_piece = lax.all_gather(incoming, 'wide', axis=0, tiled=True)  37.4 us
    all_gather x1, waiting for transfers between devices, on_device(): lax.all_gather(key_rows, 'wide', axis=0, tiled=True)  30.6 us
    all_gather x1, blocking collectives, on_device(): lax.all_gather(log_total, 'wide', axis=1, tiled=True)  19.6 us
    all_gather x1, blocking collectives, on_device(): lax.all_gather(row_delta, 'wide', axis=1, tiled=True)  18.5 us
    all_to_all x1, blocking collectives, on_device(): lax.all_to_all(grouped, 'narrow', split_axis=1, concat_axis=0, tiled=True)  13.4 us
    dot_general x1, matrix products, on_device(): jnp.einsum('hqk,qhd->khd', score_grad, query_split, preferred_element_typ...  7.27 us
    all_gather x1, local copies, waits for them, and re-layouts, on_device(): query_piece = lax.all_gather(query_rows, 'wide', axis=0, tiled=True)  6.45 us
  transfers between devices with their start and end apart: 4, of which 3 were waited for; matrix products, arithmetic and copies ran while one was open for 16% of the time, Pallas kernels for 0%

commit v1 on v0

--- a/solution.py
+++ b/solution.py
@@ -90,7 +90,12 @@
         lax.all_gather(row_delta, "wide", axis=1, tiled=True),
     )
     query_piece = lax.all_gather(query_rows, "wide", axis=0, tiled=True)
-    grad_piece = lax.all_gather(incoming, "wide", axis=0, tiled=True)
+    ring = [incoming]
+    for hop in range(15):
+        ring.append(lax.ppermute(ring[-1], "wide", [(dev, (dev + 1) % 16) for dev in range(16)]))
+    grad_piece = jnp.roll(
+        jnp.concatenate(ring[::-1], axis=0), (lax.axis_index("wide") + 1) * ring[0].shape[0], axis=0
+    )
     piece_rows = query_piece.shape[0]
     query_split = query_piece.reshape(piece_rows, heads_here, HD)
     grad_split = grad_piece.reshape(piece_rows, heads_here, HD)

time: 241 us -> 301 us (1.25)
  waiting for transfers between devices: 114 us -> 143 us
  local copies, waits for them, and re-layouts: 36.1 us -> 64.5 us
    ppermute x0 -> x15, waiting for transfers between devices: none -> 142 us  [on_device(): lax.ppermute(ring[-1], 'wide', [(dev, (dev + 1) % 16) for dev in range(16)])]
    all_gather x1, waiting for transfers between devices: 43.6 us -> 0.01 us  [on_device(): lax.all_gather(value_rows, 'wide', axis=0, tiled=True)]
    all_gather x1 -> x0, waiting for transfers between devices: 37.4 us -> none  [on_device(): grad_piece = lax.all_gather(incoming, 'wide', axis=0, tiled=True)]
    all_gather x1, waiting for transfers between devices: 30.6 us -> 0.01 us  [on_device(): lax.all_gather(key_rows, 'wide', axis=0, tiled=True)]
    unnamed x16 -> x97, local copies, waits for them, and re-layouts: 1.19 us -> 26.5 us
    dynamic_slice x0 -> x2, local copies, waits for them, and re-layouts: none -> 9.27 us  [on_device(): jnp.roll(jnp.concatenate(ring[::-1], axis=0), (lax.axis_index('wide') + 1...]
    all_gather x1 -> x0, local copies, waits for them, and re-layouts: 6.29 us -> none  [on_device(): grad_piece = lax.all_gather(incoming, 'wide', axis=0, tiled=True)]
  transfers between devices with their start and end apart: 4 -> 18, of which waited for: 3 -> 15; matrix products, arithmetic and copies ran while one was open for 16% -> 19% of each run, Pallas kernels for 0% -> 0%
where the time goes in v1:
time: 301 us; the launch traced here: 300 us
  waiting for transfers between devices  143 us (48%)
  local copies, waits for them, and re-layouts  64.5 us (21%)
  blocking collectives  50.9 us (17%)
  matrix products  25.9 us (9%)
  between operations  14.3 us (5%)
    ppermute x15, waiting for transfers between devices, on_device(): lax.ppermute(ring[-1], 'wide', [(dev, (dev + 1) % 16) for dev in range(16)])  142 us
    unnamed x97, local copies, waits for them, and re-layouts  26.5 us
    all_gather x1, blocking collectives, on_device(): lax.all_gather(row_delta, 'wide', axis=1, tiled=True)  19.8 us
    all_gather x1, blocking collectives, on_device(): lax.all_gather(log_total, 'wide', axis=1, tiled=True)  17.6 us
    all_to_all x1, blocking collectives, on_device(): lax.all_to_all(grouped, 'narrow', split_axis=1, concat_axis=0, tiled=True)  13.4 us
    dynamic_slice x2, local copies, waits for them, and re-layouts, on_device(): jnp.roll(jnp.concatenate(ring[::-1], axis=0), (lax.axis_index('wide') + 1...  9.27 us
    dot_general x1, matrix products, on_device(): jnp.einsum('hqk,qhd->khd', score_grad, query_split, preferred_element_typ...  7.28 us
    all_gather x1, local copies, waits for them, and re-layouts, on_device(): lax.all_gather(value_rows, 'wide', axis=0, tiled=True)  6.3 us
  transfers between devices with their start and end apart: 18, of which 15 were waited for; matrix products, arithmetic and copies ran while one was open for 19% of the time, Pallas kernels for 0%

profile of v1, /device:TPU:0, one launch (start us, length us, event | category | flops | bytes accessed | tf_op | source)
XLA Modules:
  0.0 300.1 jit_solution(583630859445377734)
XLA Ops:
  8.7 2.4 reshape.125
  12.5 13.4 %all_to_all.15 = bf16[20,2,4,2048]{3,2,0,1:T(4,128)(2,1)S(1)} all-to-all(bf16[20,2,4,2048]{3,2,0,1:T(4,128)(2,1)S(1)} %copy.35), channel_id=1, replica_groups=mesh['wide'=16,'narrow'=2] {'narrow'}, dimensions={1} | all-to-all | bytes 1310720 | tf_op jit(solution)/shard_map/all_to_all | solution.py:22
  27.5 10.0 %collective-permute-done = bf16[40,3072]{1,0:T(8,128)(2,1)S(1)} collective-permute-done((bf16[40,3072]{1,0:T(8,128)(2,1)S(1)}, bf16[40,3072]{1,0:T(8,128)(2,1)S(1)}, u32[]{:S(2)}, u32[]{:S(2)}) %collective-permute-start) | collective-permute-done | bytes 245792 | tf_op jit(solution)/shard_map/ppermute | solution.py:95
  38.1 11.5 %collective-permute-done.1 = bf16[40,3072]{1,0:T(8,128)(2,1)S(1)} collective-permute-done((bf16[40,3072]{1,0:T(8,128)(2,1)S(1)}, bf16[40,3072]{1,0:T(8,128)(2,1)S(1)}, u32[]{:S(2)}, u32[]{:S(2)}) %collective-permute-start.1) | collective-permute-done | bytes 245792 | tf_op jit(solution)/shard_map/ppermute | solution.py:95
  50.4 10.3 %collective-permute-done.2 = bf16[40,3072]{1,0:T(8,128)(2,1)S(1)} collective-permute-done((bf16[40,3072]{1,0:T(8,128)(2,1)S(1)}, bf16[40,3072]{1,0:T(8,128)(2,1)S(1)}, u32[]{:S(2)}, u32[]{:S(2)}) %collective-permute-start.2) | collective-permute-done | bytes 245792 | tf_op jit(solution)/shard_map/ppermute | solution.py:95
  61.4 8.3 %collective-permute-done.3 = bf16[40,3072]{1,0:T(8,128)(2,1)S(1)} collective-permute-done((bf16[40,3072]{1,0:T(8,128)(2,1)S(1)}, bf16[40,3072]{1,0:T(8,128)(2,1)S(1)}, u32[]{:S(2)}, u32[]{:S(2)}) %collective-permute-start.3) | collective-permute-done | bytes 245792 | tf_op jit(solution)/shard_map/ppermute | solution.py:95
  70.4 8.4 %collective-permute-done.4 = bf16[40,3072]{1,0:T(8,128)(2,1)S(1)} collective-permute-done((bf16[40,3072]{1,0:T(8,128)(2,1)S(1)}, bf16[40,3072]{1,0:T(8,128)(2,1)S(1)}, u32[]{:S(2)}, u32[]{:S(2)}) %collective-permute-start.4) | collective-permute-done | bytes 245792 | tf_op jit(solution)/shard_map/ppermute | solution.py:95
  79.5 12.1 %collective-permute-done.5 = bf16[40,3072]{1,0:T(8,128)(2,1)S(1)} collective-permute-done((bf16[40,3072]{1,0:T(8,128)(2,1)S(1)}, bf16[40,3072]{1,0:T(8,128)(2,1)S(1)}, u32[]{:S(2)}, u32[]{:S(2)}) %collective-permute-start.5) | collective-permute-done | bytes 245792 | tf_op jit(solution)/shard_map/ppermute | solution.py:95
  92.3 10.5 %collective-permute-done.6 = bf16[40,3072]{1,0:T(8,128)(2,1)S(1)} collective-permute-done((bf16[40,3072]{1,0:T(8,128)(2,1)S(1)}, bf16[40,3072]{1,0:T(8,128)(2,1)S(1)}, u32[]{:S(2)}, u32[]{:S(2)}) %collective-permute-start.6) | collective-permute-done | bytes 245792 | tf_op jit(solution)/shard_map/ppermute | solution.py:95
  103.5 12.1 %collective-permute-done.7 = bf16[40,3072]{1,0:T(8,128)(2,1)S(1)} collective-permute-done((bf16[40,3072]{1,0:T(8,128)(2,1)S(1)}, bf16[40,3072]{1,0:T(8,128)(2,1)S(1)}, u32[]{:S(2)}, u32[]{:S(2)}) %collective-permute-start.7) | collective-permute-done | bytes 245792 | tf_op jit(solution)/shard_map/ppermute | solution.py:95
  116.3 8.3 %collective-permute-done.8 = bf16[40,3072]{1,0:T(8,128)(2,1)S(1)} collective-permute-done((bf16[40,3072]{1,0:T(8,128)(2,1)S(1)}, bf16[40,3072]{1,0:T(8,128)(2,1)S(1)}, u32[]{:S(2)}, u32[]{:S(2)}) %collective-permute-start.8) | collective-permute-done | bytes 245792 | tf_op jit(solution)/shard_map/ppermute | solution.py:95
  125.4 7.6 %collective-permute-done.9 = bf16[40,3072]{1,0:T(8,128)(2,1)S(1)} collective-permute-done((bf16[40,3072]{1,0:T(8,128)(2,1)S(1)}, bf16[40,3072]{1,0:T(8,128)(2,1)S(1)}, u32[]{:S(2)}, u32[]{:S(2)}) %collective-permute-start.9) | collective-permute-done | bytes 245792 | tf_op jit(solution)/shard_map/ppermute | solution.py:95
  133.7 8.3 %collective-permute-done.10 = bf16[40,3072]{1,0:T(8,128)(2,1)S(1)} collective-permute-done((bf16[40,3072]{1,0:T(8,128)(2,1)S(1)}, bf16[40,3072]{1,0:T(8,128)(2,1)S(1)}, u32[]{:S(2)}, u32[]{:S(2)}) %collective-permute-start.10) | collective-permute-done | bytes 245792 | tf_op jit(solution)/shard_map/ppermute | solution.py:95
  142.7 8.3 %collective-permute-done.11 = bf16[40,3072]{1,0:T(8,128)(2,1)S(1)} collective-permute-done((bf16[40,3072]{1,0:T(8,128)(2,1)S(1)}, bf16[40,3072]{1,0:T(8,128)(2,1)S(1)}, u32[]{:S(2)}, u32[]{:S(2)}) %collective-permute-start.11) | collective-permute-done | bytes 245792 | tf_op jit(solution)/shard_map/ppermute | solution.py:95
  151.7 8.4 %collective-permute-done.12 = bf16[40,3072]{1,0:T(8,128)(2,1)} collective-permute-done((bf16[40,3072]{1,0:T(8,128)(2,1)S(1)}, bf16[40,3072]{1,0:T(8,128)(2,1)}, u32[]{:S(2)}, u32[]{:S(2)}) %collective-permute-start.12) | collective-permute-done | bytes 245792 | tf_op jit(solution)/shard_map/ppermute | solution.py:95
  160.2 8.6 %collective-permute-done.13 = bf16[40,3072]{1,0:T(8,128)(2,1)} collective-permute-done((bf16[40,3072]{1,0:T(8,128)(2,1)}, bf16[40,3072]{1,0:T(8,128)(2,1)}, u32[]{:S(2)}, u32[]{:S(2)}) %collective-permute-start.13) | collective-permute-done | bytes 245792 | tf_op jit(solution)/shard_map/ppermute | solution.py:95
  169.6 1.7 copy.37
  173.1 9.3 %collective-permute-done.14 = bf16[40,3072]{1,0:T(8,128)(2,1)} collective-permute-done((bf16[40,3072]{1,0:T(8,128)(2,1)}, bf16[40,3072]{1,0:T(8,128)(2,1)}, u32[]{:S(2)}, u32[]{:S(2)}) %collective-permute-start.14) | collective-permute-done | bytes 245792 | tf_op jit(solution)/shard_map/ppermute | solution.py:95
  200.5 2.9 constant_dynamic-slice_fusion
  203.4 6.4 %copy.48 = bf16[640,3072]{0,1:T(8,128)(2,1)} copy(bf16[640,3072]{1,0:T(8,128)(2,1)} %constant_dynamic-slice_fusion) | data formatting | bytes 7864320 | tf_op jit(solution)/shard_map/jit(_roll_dynamic)/dynamic_slice | solution.py:96
  209.7 6.3 %copy.32 = bf16[640,3072]{0,1:T(8,128)(2,1)} copy(bf16[640,3072]{1,0:T(8,128)(2,1)} %all-gather.6.cloned.1.call-done) | data formatting | bytes 7864320 | tf_op jit(solution)/shard_map/all_gather | solution.py:42
  216.0 6.3 %copy.38 = bf16[640,3072]{0,1:T(8,128)(2,1)} copy(bf16[640,3072]{1,0:T(8,128)(2,1)} %all-gather.8.cloned.1.call-done) | data formatting | bytes 7864320 | tf_op jit(solution)/shard_map/all_gather | solution.py:43
  222.3 3.2 %fusion.57 = (f32[24,40]{1,0:T(8,128)S(1)}, f32[24,40,640]{2,1,0:T(8,128)S(1)}) fusion(bf16[640,24,128]{0,2,1:T(8,128)(2,1)} %bitcast.76, pred[40,640]{1,0:T(8,128)(4,1)S(1)} %iota_compare_fusion.1, bf16[40,3072]{1,0:T(8,128)(2,1)S(1)} %copy-done.3), kind=kOutput, calls=%fused_computation.95 | convolution fusion | flops 159128640 | bytes 6664960 | tf_op jit(solution)/shard_map/qhd,khd->hqk/dot_general | solution.py:74
  225.6 2.5 fusion.2
  228.1 1.8 fusion.33
  230.7 6.2 %copy.43 = bf16[640,3072]{0,1:T(8,128)(2,1)} copy(bf16[640,3072]{1,0:T(8,128)(2,1)} %all-gather.10.cloned.1.call-done) | data formatting | bytes 7864320 | tf_op jit(solution)/shard_map/all_gather | solution.py:92
  236.9 4.3 %fusion.43 = f32[24,640,40]{1,2,0:T(8,128)} fusion(bf16[640,24,128]{0,2,1:T(8,128)(2,1)} %bitcast.78, bf16[40,3072]{1,0:T(8,128)(2,1)S(1)} %copy-done.4), kind=kOutput, calls=%fused_computation.43 | convolution fusion | flops 157286400 | bytes 6635520 | tf_op jit(solution)/shard_map/qhd,khd->hqk/dot_general | solution.py:105
  241.2 17.6 %all-gather = f32[16,40,24]{1,2,0:T(8,128)S(1)} all-gather(f32[1,40,24]{1,2,0:T(8,128)S(1)} %bitcast.90), channel_id=1, replica_groups=mesh['wide'=16,'narrow'=2] {'wide'}, dimensions={0}, use_global_device_ids=true | all-gather | bytes 65280 | tf_op jit(solution)/shard_map/all_gather | solution.py:89
  259.0 19.8 %all-gather.1 = f32[16,40,24]{1,2,0:T(8,128)S(1)} all-gather(f32[1,40,24]{1,2,0:T(8,128)S(1)} %bitcast.89), channel_id=1, replica_groups=mesh['wide'=16,'narrow'=2] {'wide'}, dimensions={0}, use_global_device_ids=true | all-gather | bytes 65280 | tf_op jit(solution)/shard_map/all_gather | solution.py:90
  279.1 5.3 %fusion.35 = bf16[24,5,8,128]{3,2,1,0:T(8,128)(2,1)} fusion(bf16[640,24,128]{0,2,1:T(8,128)(2,1)} %bitcast.81, f32[24,640,40]{1,2,0:T(8,128)} %fusion.43, f32[24,640]{1,0:T(8,128)S(1)} %bitcast.91, pred[640,40]{0,1:T(8,128)(4,1)S(1)} %copy-done.31), kind=kOutput, calls=%fused_computation.36 | convolution fusion | flops 160481280 | bytes 6722560 | tf_op jit(solution)/shard_map/hqk,qhd->khd/dot_general | solution.py:117
  284.4 7.3 %fusion.34 = bf16[24,5,8,128]{3,2,1,0:T(8,128)(2,1)} fusion(bf16[640,24,128]{0,2,1:T(8,128)(2,1)} %bitcast.79, f32[24,640,40]{1,2,0:T(8,128)} %fusion.43, bf16[640,24,128]{0,2,1:T(8,128)(2,1)} %bitcast.82, f32[24,640]{1,0:T(8,128)S(1)} %bitcast.93, f32[24,640]{1,0:T(8,128)S(1)} %bitcast.92, pred[640,40]{0,1:T(8,128)(4,1)S(1)} %copy-done.31, ...), kind=kOutput, calls=%fused_computation.35 | convolution fusion | flops 319119360 | bytes 10961920 | tf_op jit(solution)/shard_map/hqk,qhd->khd/dot_general | solution.py:114
  291.7 1.9 copy_bitcast_fusion
  (134 shorter events, 34.4 us)
Async XLA Ops:
  7.2 202.6 %all-gather.6.cloned.1.call-start = ((), (), s32[]{:S(2)}) async-start(), calls=%async_computation.1 | async-start | bytes 4177920 | tf_op jit(solution)/shard_map/all_gather | solution.py:42
  7.9 208.1 %all-gather.8.cloned.1.call-start = ((), (), s32[]{:S(2)}) async-start(), calls=%async_computation.2 | async-start | bytes 4177920 | tf_op jit(solution)/shard_map/all_gather | solution.py:43
  8.7 222.0 %all-gather.10.cloned.1.call-start = ((), (), s32[]{:S(2)}) async-start(), calls=%async_computation.3 | async-start | bytes 4177920 | tf_op jit(solution)/shard_map/all_gather | solution.py:92
  27.4 97.3 %copy-start.21 = (bf16[40,4,768]{2,0,1:T(8,128)(2,1)}, bf16[40,4,768]{2,0,1:T(8,128)(2,1)S(1)}, u32[]{:S(2)}) copy-start(bf16[40,4,768]{2,0,1:T(8,128)(2,1)S(1)} %fusion.25) | copy-start | bytes 737284
  27.4 10.0 %collective-permute-start = (bf16[40,3072]{1,0:T(8,128)(2,1)S(1)}, bf16[40,3072]{1,0:T(8,128)(2,1)S(1)}, u32[]{:S(2)}, u32[]{:S(2)}) collective-permute-start(bf16[40,3072]{1,0:T(8,128)(2,1)S(1)} %bitcast.83), channel_id=1, source_target_pairs={{0,2},{2,4},{4,6},{6,8},{8,10},{10,12},{12,14},{14,16},{16,18},{18... | collective-permute-start | bytes 737288 | tf_op jit(solution)/shard_map/ppermute | solution.py:95
  38.1 11.5 %collective-permute-start.1 = (bf16[40,3072]{1,0:T(8,128)(2,1)S(1)}, bf16[40,3072]{1,0:T(8,128)(2,1)S(1)}, u32[]{:S(2)}, u32[]{:S(2)}) collective-permute-start(bf16[40,3072]{1,0:T(8,128)(2,1)S(1)} %collective-permute-done), channel_id=1, source_target_pairs={{0,2},{2,4},{4,6},{6,8},{8,10},{10,12},{12,14},{14,16},{16,18},{18... | collective-permute-start | bytes 737288 | tf_op jit(solution)/shard_map/ppermute | solution.py:95
  50.4 10.3 %collective-permute-start.2 = (bf16[40,3072]{1,0:T(8,128)(2,1)S(1)}, bf16[40,3072]{1,0:T(8,128)(2,1)S(1)}, u32[]{:S(2)}, u32[]{:S(2)}) collective-permute-start(bf16[40,3072]{1,0:T(8,128)(2,1)S(1)} %collective-permute-done.1), channel_id=1, source_target_pairs={{0,2},{2,4},{4,6},{6,8},{8,10},{10,12},{12,14},{14,16},{16,18},{18... | collective-permute-start | bytes 737288 | tf_op jit(solution)/shard_map/ppermute | solution.py:95
  61.4 8.3 %collective-permute-start.3 = (bf16[40,3072]{1,0:T(8,128)(2,1)S(1)}, bf16[40,3072]{1,0:T(8,128)(2,1)S(1)}, u32[]{:S(2)}, u32[]{:S(2)}) collective-permute-start(bf16[40,3072]{1,0:T(8,128)(2,1)S(1)} %collective-permute-done.2), channel_id=1, source_target_pairs={{0,2},{2,4},{4,6},{6,8},{8,10},{10,12},{12,14},{14,16},{16,18},{18... | collective-permute-start | bytes 737288 | tf_op jit(solution)/shard_map/ppermute | solution.py:95
  70.4 8.4 %collective-permute-start.4 = (bf16[40,3072]{1,0:T(8,128)(2,1)S(1)}, bf16[40,3072]{1,0:T(8,128)(2,1)S(1)}, u32[]{:S(2)}, u32[]{:S(2)}) collective-permute-start(bf16[40,3072]{1,0:T(8,128)(2,1)S(1)} %collective-permute-done.3), channel_id=1, source_target_pairs={{0,2},{2,4},{4,6},{6,8},{8,10},{10,12},{12,14},{14,16},{16,18},{18... | collective-permute-start | bytes 737288 | tf_op jit(solution)/shard_map/ppermute | solution.py:95
  79.5 12.1 %collective-permute-start.5 = (bf16[40,3072]{1,0:T(8,128)(2,1)S(1)}, bf16[40,3072]{1,0:T(8,128)(2,1)S(1)}, u32[]{:S(2)}, u32[]{:S(2)}) collective-permute-start(bf16[40,3072]{1,0:T(8,128)(2,1)S(1)} %collective-permute-done.4), channel_id=1, source_target_pairs={{0,2},{2,4},{4,6},{6,8},{8,10},{10,12},{12,14},{14,16},{16,18},{18... | collective-permute-start | bytes 737288 | tf_op jit(solution)/shard_map/ppermute | solution.py:95
  92.3 10.5 %collective-permute-start.6 = (bf16[40,3072]{1,0:T(8,128)(2,1)S(1)}, bf16[40,3072]{1,0:T(8,128)(2,1)S(1)}, u32[]{:S(2)}, u32[]{:S(2)}) collective-permute-start(bf16[40,3072]{1,0:T(8,128)(2,1)S(1)} %collective-permute-done.5), channel_id=1, source_target_pairs={{0,2},{2,4},{4,6},{6,8},{8,10},{10,12},{12,14},{14,16},{16,18},{18... | collective-permute-start | bytes 737288 | tf_op jit(solution)/shard_map/ppermute | solution.py:95
  103.5 12.1 %collective-permute-start.7 = (bf16[40,3072]{1,0:T(8,128)(2,1)S(1)}, bf16[40,3072]{1,0:T(8,128)(2,1)S(1)}, u32[]{:S(2)}, u32[]{:S(2)}) collective-permute-start(bf16[40,3072]{1,0:T(8,128)(2,1)S(1)} %collective-permute-done.6), channel_id=1, source_target_pairs={{0,2},{2,4},{4,6},{6,8},{8,10},{10,12},{12,14},{14,16},{16,18},{18... | collective-permute-start | bytes 737288 | tf_op jit(solution)/shard_map/ppermute | solution.py:95
  116.3 8.3 %collective-permute-start.8 = (bf16[40,3072]{1,0:T(8,128)(2,1)S(1)}, bf16[40,3072]{1,0:T(8,128)(2,1)S(1)}, u32[]{:S(2)}, u32[]{:S(2)}) collective-permute-start(bf16[40,3072]{1,0:T(8,128)(2,1)S(1)} %collective-permute-done.7), channel_id=1, source_target_pairs={{0,2},{2,4},{4,6},{6,8},{8,10},{10,12},{12,14},{14,16},{16,18},{18... | collective-permute-start | bytes 737288 | tf_op jit(solution)/shard_map/ppermute | solution.py:95
  124.7 8.3 %collective-permute-start.9 = (bf16[40,3072]{1,0:T(8,128)(2,1)S(1)}, bf16[40,3072]{1,0:T(8,128)(2,1)S(1)}, u32[]{:S(2)}, u32[]{:S(2)}) collective-permute-start(bf16[40,3072]{1,0:T(8,128)(2,1)S(1)} %collective-permute-done.8), channel_id=1, source_target_pairs={{0,2},{2,4},{4,6},{6,8},{8,10},{10,12},{12,14},{14,16},{16,18},{18... | collective-permute-start | bytes 737288 | tf_op jit(solution)/shard_map/ppermute | solution.py:95
  133.7 8.3 %collective-permute-start.10 = (bf16[40,3072]{1,0:T(8,128)(2,1)S(1)}, bf16[40,3072]{1,0:T(8,128)(2,1)S(1)}, u32[]{:S(2)}, u32[]{:S(2)}) collective-permute-start(bf16[40,3072]{1,0:T(8,128)(2,1)S(1)} %collective-permute-done.9), channel_id=1, source_target_pairs={{0,2},{2,4},{4,6},{6,8},{8,10},{10,12},{12,14},{14,16},{16,18},{18... | collective-permute-start | bytes 737288 | tf_op jit(solution)/shard_map/ppermute | solution.py:95
  142.7 8.3 %collective-permute-start.11 = (bf16[40,3072]{1,0:T(8,128)(2,1)S(1)}, bf16[40,3072]{1,0:T(8,128)(2,1)S(1)}, u32[]{:S(2)}, u32[]{:S(2)}) collective-permute-start(bf16[40,3072]{1,0:T(8,128)(2,1)S(1)} %collective-permute-done.10), channel_id=1, source_target_pairs={{0,2},{2,4},{4,6},{6,8},{8,10},{10,12},{12,14},{14,16},{16,18},{18... | collective-permute-start | bytes 737288 | tf_op jit(solution)/shard_map/ppermute | solution.py:95
  151.7 8.4 %collective-permute-start.12 = (bf16[40,3072]{1,0:T(8,128)(2,1)S(1)}, bf16[40,3072]{1,0:T(8,128)(2,1)}, u32[]{:S(2)}, u32[]{:S(2)}) collective-permute-start(bf16[40,3072]{1,0:T(8,128)(2,1)S(1)} %collective-permute-done.11), channel_id=1, source_target_pairs={{0,2},{2,4},{4,6},{6,8},{8,10},{10,12},{12,14},{14,16},{16,18},{18... | collective-permute-start | bytes 737288 | tf_op jit(solution)/shard_map/ppermute | solution.py:95
  160.1 8.6 %collective-permute-start.13 = (bf16[40,3072]{1,0:T(8,128)(2,1)}, bf16[40,3072]{1,0:T(8,128)(2,1)}, u32[]{:S(2)}, u32[]{:S(2)}) collective-permute-start(bf16[40,3072]{1,0:T(8,128)(2,1)} %collective-permute-done.12), channel_id=1, source_target_pairs={{0,2},{2,4},{4,6},{6,8},{8,10},{10,12},{12,14},{14,16},{16,18},{18... | collective-permute-start | bytes 737288 | tf_op jit(solution)/shard_map/ppermute | solution.py:95
  168.8 13.7 %collective-permute-start.14 = (bf16[40,3072]{1,0:T(8,128)(2,1)}, bf16[40,3072]{1,0:T(8,128)(2,1)}, u32[]{:S(2)}, u32[]{:S(2)}) collective-permute-start(bf16[40,3072]{1,0:T(8,128)(2,1)} %collective-permute-done.13), channel_id=1, source_target_pairs={{0,2},{2,4},{4,6},{6,8},{8,10},{10,12},{12,14},{14,16},{16,18},{18... | collective-permute-start | bytes 737288 | tf_op jit(solution)/shard_map/ppermute | solution.py:95
  173.0 27.0 %copy-start.29 = (bf16[40,3072]{1,0:T(8,128)(2,1)S(1)}, bf16[40,3072]{1,0:T(8,128)(2,1)}, u32[]{:S(2)}) copy-start(bf16[40,3072]{1,0:T(8,128)(2,1)} %copy-done.28) | copy-start | bytes 737284
  173.0 27.0 %copy-start.27 = (bf16[40,3072]{1,0:T(8,128)(2,1)S(1)}, bf16[40,3072]{1,0:T(8,128)(2,1)}, u32[]{:S(2)}) copy-start(bf16[40,3072]{1,0:T(8,128)(2,1)} %copy-done.26) | copy-start | bytes 737284
  173.0 27.0 %copy-start.25 = (bf16[40,3072]{1,0:T(8,128)(2,1)S(1)}, bf16[40,3072]{1,0:T(8,128)(2,1)}, u32[]{:S(2)}) copy-start(bf16[40,3072]{1,0:T(8,128)(2,1)} %copy-done.24) | copy-start | bytes 737284
  173.0 27.1 %copy-start.23 = (bf16[40,3072]{1,0:T(8,128)(2,1)S(1)}, bf16[40,3072]{1,0:T(8,128)(2,1)}, u32[]{:S(2)}) copy-start(bf16[40,3072]{1,0:T(8,128)(2,1)} %copy-done.22) | copy-start | bytes 737284
  173.1 27.1 %copy-start.20 = (bf16[40,3072]{1,0:T(8,128)(2,1)S(1)}, bf16[40,3072]{1,0:T(8,128)(2,1)}, u32[]{:S(2)}) copy-start(bf16[40,3072]{1,0:T(8,128)(2,1)} %copy-done.19) | copy-start | bytes 737284
  173.1 27.1 %copy-start.18 = (bf16[40,3072]{1,0:T(8,128)(2,1)S(1)}, bf16[40,3072]{1,0:T(8,128)(2,1)}, u32[]{:S(2)}) copy-start(bf16[40,3072]{1,0:T(8,128)(2,1)} %copy-done.17) | copy-start | bytes 737284
  173.1 27.2 %copy-start.16 = (bf16[40,3072]{1,0:T(8,128)(2,1)S(1)}, bf16[40,3072]{1,0:T(8,128)(2,1)}, u32[]{:S(2)}) copy-start(bf16[40,3072]{1,0:T(8,128)(2,1)} %copy-done.15) | copy-start | bytes 737284
  173.1 27.2 %copy-start.14 = (bf16[40,3072]{1,0:T(8,128)(2,1)S(1)}, bf16[40,3072]{1,0:T(8,128)(2,1)}, u32[]{:S(2)}) copy-start(bf16[40,3072]{1,0:T(8,128)(2,1)} %copy-done.13) | copy-start | bytes 737284
  173.1 27.2 %copy-start.12 = (bf16[40,3072]{1,0:T(8,128)(2,1)S(1)}, bf16[40,3072]{1,0:T(8,128)(2,1)}, u32[]{:S(2)}) copy-start(bf16[40,3072]{1,0:T(8,128)(2,1)} %copy-done.11) | copy-start | bytes 737284
  173.1 27.2 %copy-start.10 = (bf16[40,3072]{1,0:T(8,128)(2,1)S(1)}, bf16[40,3072]{1,0:T(8,128)(2,1)}, u32[]{:S(2)}) copy-start(bf16[40,3072]{1,0:T(8,128)(2,1)} %copy-done.9) | copy-start | bytes 737284
  173.1 27.3 %copy-start.8 = (bf16[40,3072]{1,0:T(8,128)(2,1)S(1)}, bf16[40,3072]{1,0:T(8,128)(2,1)}, u32[]{:S(2)}) copy-start(bf16[40,3072]{1,0:T(8,128)(2,1)} %copy-done.7) | copy-start | bytes 737284
  173.1 27.3 %copy-start.6 = (bf16[40,3072]{1,0:T(8,128)(2,1)S(1)}, bf16[40,3072]{1,0:T(8,128)(2,1)}, u32[]{:S(2)}) copy-start(bf16[40,3072]{1,0:T(8,128)(2,1)} %copy-done.5) | copy-start | bytes 737284
  230.7 48.4 %copy-start.31 = (pred[640,40]{0,1:T(8,128)(4,1)S(1)}, pred[640,40]{0,1:T(8,128)(4,1)}, u32[]{:S(2)}) copy-start(pred[640,40]{0,1:T(8,128)(4,1)} %iota_compare_fusion) | copy-start | bytes 76804
  (18 other events, 63.0 us)
Sparse Core Ops, SparseCore 0:
  10.3 55.2 all-gather.5
  67.8 52.4 all-gather.7
  160.3 50.8 all-gather.9
